TPU v7x, 32 devices: a whole 2x2x4 slice. The times are simulated.
32 devices in a mesh: tile: 8 (over z, y), mem: 4 (over x, core).
Axes of the slice: x: 2, y: 2, z: 4, core: 2. Of those that a mesh axis runs over, the one named last changes fastest.
Arguments:
- control: bfloat16 [32, 16, 24576], P('mem', None, 'tile'), may hold values from -6 to 6
- ensemble: bfloat16 [32, 16, 24576], P('mem', None, 'tile'), may hold values from -1 to 1
- vertical_loc: bfloat16 [16, 16], replicated, may hold values from -1.5 to 1.5
- blocks: bfloat16 [192, 7, 128, 128], P('tile'), as said below
- edge_mask: int32 [192, 7], P('tile'), may hold values from 0 to 1, as said below
- background: float32 [16, 24576], P(None, 'tile'), may hold values from -6 to 6
- obs_precision: float32 [16, 24576], P(None, 'tile'), may hold values from 1 to 10
Outputs:
- increment: float32 [16, 24576], P('mem', 'tile')
- gradient: float32 [32, 16, 24576], P('mem', None, 'tile')
Inputs may be any that keep to these rules, and one draw needn't show every extreme that they name: `edge_mask`: each entry is 0 or 1; slot 0 is 1 for every tile; slot 2d of tile (t + d) mod 192 equals slot 2d-1 of tile t. Slot 0 blocks are symmetric, and the block in slot 2d of tile (t + d) mod 192 is the transpose of the block in slot 2d-1 of tile t, so that Lh is symmetric.
All inputs are finite; a program needn't handle non-finite values.
Results may differ from a plain program's by a relative error of at most 0.011.
Values may be sent and summed in bfloat16 or wider, within the bound.
No kernel may reach another device: no remote copies, remote signals or barrier semaphores. Data moves between devices by JAX's collectives and lax.ppermute only.
A program may use at most 64 MiB of HBM per device.

v0:
```python
import jax
import jax.numpy as jnp
from jax import lax
from jax.sharding import PartitionSpec as P


def padded_2(value, sides, width):
    for axis, dim in sides:
        size, length = (lax.axis_size(axis), value.shape[dim])
        up = [(i, (i + 1) % size) for i in range(size)]
        down = [(j, i) for i, j in up]
        last = lax.slice_in_dim(value, length - width, length, axis=dim)
        first = lax.slice_in_dim(value, 0, width, axis=dim)
        before = lax.ppermute(last, axis, up)
        after = lax.ppermute(first, axis, down)
        value = jnp.concatenate([before, value, after], axis=dim)
    return value


def passed_along(value, axis, by):
    length = lax.axis_size(axis)
    return lax.ppermute(value, axis, [(i, (i + by) % length) for i in range(length)])


def slot_offset(slot_index):
    if slot_index == 0:
        return 0
    distance = (slot_index + 1) // 2
    if slot_index % 2 == 1:
        return distance
    return -distance


def apply_rows(padded, blocks, edge_mask, tile_count):
    member_count, level_count, padded_points = padded.shape
    block_width = blocks.shape[-1]
    padded_tiles = padded.reshape(
        member_count, level_count, padded_points // block_width, block_width
    )
    reach_tiles = (padded_points // block_width - tile_count) // 2
    mask_float = edge_mask.astype(jnp.float32)
    summed = jnp.zeros((member_count, level_count, tile_count, block_width), jnp.float32)
    for slot_index in range(blocks.shape[1]):
        offset = slot_offset(slot_index)
        source = padded_tiles[:, :, reach_tiles + offset : reach_tiles + offset + tile_count]
        product = jnp.einsum(
            "tab,kltb->klta", blocks[:, slot_index], source, preferred_element_type=jnp.float32
        )
        summed = summed + mask_float[None, None, :, slot_index, None] * product
    return summed


def on_device(control, ensemble, vertical_loc, blocks, edge_mask, background, obs_precision):
    member_count, level_count, point_count = control.shape
    block_width = blocks.shape[-1]
    tile_count = point_count // block_width
    reach_tiles = (blocks.shape[1] - 1) // 2
    vertical = jnp.einsum(
        "lm,kmh->klh", vertical_loc, control, preferred_element_type=jnp.float32
    ).astype(jnp.bfloat16)
    padded = padded_2(vertical, (("tile", 2),), reach_tiles * block_width)
    localized = apply_rows(padded, blocks, edge_mask, tile_count).reshape(
        member_count, level_count, point_count
    )
    partial_sum = jnp.sum(ensemble.astype(jnp.float32) * localized, axis=0)
    row_count = level_count // lax.axis_size("mem")
    first_row = lax.axis_index("mem") * row_count
    summed_total = lax.psum(partial_sum, "mem")
    increment = lax.dynamic_slice_in_dim(summed_total, first_row, row_count, 0)
    depart = (obs_precision * (summed_total - background)).astype(jnp.bfloat16)
    weighted = (ensemble.astype(jnp.float32) * depart.astype(jnp.float32)[None]).astype(
        jnp.bfloat16
    )
    weighted_tiles = weighted.reshape(member_count, level_count, tile_count, block_width)
    mask_float = edge_mask.astype(jnp.float32)
    extended = jnp.zeros(
        (member_count, level_count, tile_count + 2 * reach_tiles, block_width), jnp.float32
    )
    for slot_index in range(blocks.shape[1]):
        offset = slot_offset(slot_index)
        contrib = jnp.einsum(
            "tab,klta->kltb",
            blocks[:, slot_index],
            weighted_tiles,
            preferred_element_type=jnp.float32,
        )
        contrib = mask_float[None, None, :, slot_index, None] * contrib
        extended = extended.at[:, :, reach_tiles + offset : reach_tiles + offset + tile_count].add(
            contrib
        )
    left_rim = extended[:, :, :reach_tiles]
    right_rim = extended[:, :, reach_tiles + tile_count :]
    from_left = passed_along(right_rim, "tile", 1)
    from_right = passed_along(left_rim, "tile", -1)
    interior = extended[:, :, reach_tiles : reach_tiles + tile_count]
    interior = interior.at[:, :, :reach_tiles].add(from_left)
    interior = interior.at[:, :, tile_count - reach_tiles :].add(from_right)
    adjoint = interior.reshape(member_count, level_count, point_count)
    gradient = control.astype(jnp.float32) + jnp.einsum(
        "ml,kmh->klh", vertical_loc.astype(jnp.float32), adjoint, precision=lax.Precision.HIGHEST
    )
    return (increment, gradient)


def solution(mesh):
    in_specs = (
        P("mem", None, "tile"),
        P("mem", None, "tile"),
        P(),
        P("tile", None, None, None),
        P("tile", None),
        P(None, "tile"),
        P(None, "tile"),
    )
    out_specs = (P("mem", "tile"), P("mem", None, "tile"))
    return jax.shard_map(
        on_device, mesh=mesh, in_specs=in_specs, out_specs=out_specs, check_vma=False
    )
```

profile of v0, /device:TPU:0, one launch (start us, length us, event | category | flops | bytes accessed | tf_op | source)
XLA Modules:
  0.0 100.6 jit_solution(4137713650633322076)
XLA Ops:
  7.2 0.0 copy-start
  7.2 0.0 copy-start.5
  7.2 0.0 all-reduce.3.cloned.1.call-start
  7.2 0.6 copy-done
  7.9 1.5 %fusion.1 = bf16[8,16,3072]{2,1,0:T(8,128)(2,1)S(1)} fusion(bf16[8,16,3072]{2,1,0:T(8,128)(2,1)} %param.25, bf16[16,16]{1,0:T(8,128)(2,1)S(1)} %copy-done), kind=kOutput, calls=%fused_computation.3 | convolution fusion | flops 12976128 | bytes 1573376 | tf_op jit(solution)/shard_map/lm,kmh->klh/dot_general | solution.py:58
  9.4 3.0 %collective-permute-start = (bf16[8,16,384]{2,1,0:T(8,128)(2,1)S(1)}, bf16[8,16,384]{2,1,0:T(8,128)(2,1)S(1)}, u32[]{:S(2)}, u32[]{:S(2)}) collective-permute-start(bf16[8,16,384]{2,1,0:T(8,128)(2,1)S(1)} %get-tuple-element.119), channel_id=1, source_target_pairs={{0,4},{4,8},{8,12},{12,16},{16,20},{20,24},{24,28},{28,0},{1,5},{5... | collective-permute-start | bytes 294920 | tf_op jit(solution)/shard_map/ppermute | solution.py:14
  12.4 3.1 %collective-permute-start.1 = (bf16[8,16,384]{2,1,0:T(8,128)(2,1)S(1)}, bf16[8,16,384]{2,1,0:T(8,128)(2,1)S(1)}, u32[]{:S(2)}, u32[]{:S(2)}) collective-permute-start(bf16[8,16,384]{2,1,0:T(8,128)(2,1)S(1)} %get-tuple-element.120), channel_id=1, source_target_pairs={{4,0},{8,4},{12,8},{16,12},{20,16},{24,20},{28,24},{0,28},{5,1},{9... | collective-permute-start | bytes 294920 | tf_op jit(solution)/shard_map/ppermute | solution.py:15
  15.5 0.0 copy-done.5
  15.5 2.8 %collective-permute-done = bf16[8,16,384]{2,1,0:T(8,128)(2,1)S(1)} collective-permute-done((bf16[8,16,384]{2,1,0:T(8,128)(2,1)S(1)}, bf16[8,16,384]{2,1,0:T(8,128)(2,1)S(1)}, u32[]{:S(2)}, u32[]{:S(2)}) %collective-permute-start) | collective-permute-done | bytes 98336 | tf_op jit(solution)/shard_map/ppermute | solution.py:14
  18.3 0.8 collective-permute-done.1
  19.1 0.1 pad_maximum_fusion
  19.2 0.6 reshape.325
  19.8 1.4 %fusion.73 = (bf16[8,16,24,128]{3,2,1,0:T(8,128)(2,1)S(1)}, bf16[8,16,24,128]{3,2,1,0:T(8,128)(2,1)S(1)}, bf16[8,16,24,128]{3,2,1,0:T(8,128)(2,1)S(1)}, bf16[8,1...) fusion(bf16[8,16,30,128]{3,2,1,0:T(8,128)(2,1)S(1)} %reshape.325), kind=kLoop, calls=%fused_computation.98 | loop fusion | bytes 11010048 | tf_op jit(solution)/shard_map/slice | solution.py:45
  21.2 1.8 %fusion.22 = f32[24,8,16,128]{3,2,1,0:T(8,128)S(1)} fusion(bf16[8,16,24,128]{3,2,1,0:T(8,128)(2,1)S(1)} %get-tuple-element.113, bf16[24,7,128,128]{3,2,1,0:T(8,128)(2,1)} %param.28), kind=kOutput, calls=%fused_computation.35 | convolution fusion | flops 100663296 | bytes 3145728 | tf_op jit(solution)/shard_map/tab,kltb->klta/dot_general | solution.py:46
  23.0 1.8 %fusion.25 = f32[24,8,16,128]{3,2,1,0:T(8,128)S(1)} fusion(bf16[8,16,24,128]{3,2,1,0:T(8,128)(2,1)S(1)} %get-tuple-element.114, bf16[24,7,128,128]{3,2,1,0:T(8,128)(2,1)} %param.28), kind=kOutput, calls=%fused_computation.38 | convolution fusion | flops 100663296 | bytes 3145728 | tf_op jit(solution)/shard_map/tab,kltb->klta/dot_general | solution.py:46
  24.8 1.8 %fusion.28 = f32[24,8,16,128]{3,2,1,0:T(8,128)S(1)} fusion(bf16[8,16,24,128]{3,2,1,0:T(8,128)(2,1)S(1)} %get-tuple-element.115, bf16[24,7,128,128]{3,2,1,0:T(8,128)(2,1)} %param.28), kind=kOutput, calls=%fused_computation.41 | convolution fusion | flops 100663296 | bytes 3145728 | tf_op jit(solution)/shard_map/tab,kltb->klta/dot_general | solution.py:46
  26.6 1.8 %fusion.31 = f32[24,8,16,128]{3,2,1,0:T(8,128)S(1)} fusion(bf16[8,16,24,128]{3,2,1,0:T(8,128)(2,1)S(1)} %get-tuple-element.116, bf16[24,7,128,128]{3,2,1,0:T(8,128)(2,1)} %param.28), kind=kOutput, calls=%fused_computation.44 | convolution fusion | flops 100663296 | bytes 3145728 | tf_op jit(solution)/shard_map/tab,kltb->klta/dot_general | solution.py:46
  28.4 1.8 %fusion.34 = f32[24,8,16,128]{3,2,1,0:T(8,128)S(1)} fusion(bf16[8,16,24,128]{3,2,1,0:T(8,128)(2,1)S(1)} %get-tuple-element.117, bf16[24,7,128,128]{3,2,1,0:T(8,128)(2,1)} %param.28), kind=kOutput, calls=%fused_computation.47 | convolution fusion | flops 100663296 | bytes 3145728 | tf_op jit(solution)/shard_map/tab,kltb->klta/dot_general | solution.py:46
  30.2 1.8 %fusion.37 = f32[24,8,16,128]{3,2,1,0:T(8,128)S(1)} fusion(bf16[8,16,24,128]{3,2,1,0:T(8,128)(2,1)S(1)} %get-tuple-element.118, bf16[24,7,128,128]{3,2,1,0:T(8,128)(2,1)} %param.28), kind=kOutput, calls=%fused_computation.50 | convolution fusion | flops 100663296 | bytes 3145728 | tf_op jit(solution)/shard_map/tab,kltb->klta/dot_general | solution.py:46
  32.0 0.0 copy-start.1
  32.0 2.3 %add_bitcast_fusion = f32[24,8,2,8,128]{4,3,2,1,0:T(8,128)S(1)} fusion(f32[24,8,16,128]{3,2,1,0:T(8,128)S(1)} %fusion.22, f32[24,8,16,128]{3,2,1,0:T(8,128)S(1)} %fusion.25, f32[24,8,16,128]{3,2,1,0:T(8,128)S(1)} %fusion.28, f32[24,8,16,128]{3,2,1,0:T(8,128)S(1)} %fusion.31, f32[24,8,16,128]{3,2,1,0:T(8,128)S(1)} %fusion.34, ...), kind=kOutput, calls=%fused_computation.21 | convolution fusion | flops 105775104 | bytes 12583584 | tf_op jit(solution)/shard_map/tab,kltb->klta/dot_general | solution.py:46
  34.3 0.0 copy-done.1
  34.3 0.0 copy-start.3
  34.4 0.0 copy-start.4
  34.4 0.9 fusion.2
  35.3 0.0 all-reduce.3.cloned.1.call-update
  35.3 32.3 %all-reduce.3.cloned.1.call-done = f32[16,3072]{1,0:T(8,128)} async-done(((f32[16,3072]{1,0:T(8,128)}), f32[16,3072]{1,0:T(8,128)}) %all-reduce.3.cloned.1.call-update) | async-done | bytes 196624 | tf_op jit(solution)/shard_map/psum | solution.py:68
  67.6 0.0 copy-done.3
  67.6 0.0 copy-done.4
  67.6 1.0 fusion.69
  68.6 0.0 slice-start
  68.6 1.7 %multiply_bitcast_fusion = f32[8,16,24,128]{3,1,0,2:T(8,128)S(1)} fusion(f32[24]{0:T(128)S(1)} %get-tuple-element.121, bf16[24,7,128,128]{3,2,1,0:T(8,128)(2,1)} %param.28, bf16[8,16,3072]{2,1,0:T(8,128)(2,1)S(1)} %copy-done.1, f32[16,3072]{1,0:T(8,128)S(1)} %fusion.69), kind=kOutput, calls=%fused_computation.22 | convolution fusion | flops 102236160 | bytes 3342432 | tf_op jit(solution)/shard_map/tab,klta->kltb/dot_general | solution.py:81
  70.3 0.0 slice-start.1
  70.3 0.2 scatter-add.30
  70.5 1.8 %fusion.10 = f32[8,16,30,128]{3,1,0,2:T(8,128)S(1)} fusion(f32[8,16,30,128]{3,1,0,2:T(8,128)S(1)} %scatter-add.30, f32[24]{0:T(128)S(1)} %get-tuple-element.127, bf16[24,7,128,128]{3,2,1,0:T(8,128)(2,1)} %param.28, bf16[8,16,3072]{2,1,0:T(8,128)(2,1)S(1)} %copy-done.1, f32[16,3072]{1,0:T(8,128)S(1)} %fusion.69), kind=kOutput, calls=%fused_computation.20 | convolution fusion | flops 102629376 | bytes 4915712 | tf_op jit(solution)/shard_map/tab,klta->kltb/dot_general | solution.py:81
  72.3 0.0 slice-done
  72.3 0.0 slice-done.1
  72.3 0.5 fusion.9
  72.9 0.5 fusion.8
  73.4 0.5 fusion.7
  74.0 0.5 fusion.6
  74.5 1.8 %constant_dynamic-update-slice_fusion = (f32[8,16,30,128]{3,1,0,2:T(8,128)S(1)}, f32[8,16,24,128]{3,1,0,2:T(8,128)}) fusion(f32[8,16,30,128]{3,1,0,2:T(8,128)S(1)} %fusion.6, bf16[24,7,128,128]{3,2,1,0:T(8,128)(2,1)S(1)} %bitcast.161, f32[24]{0:T(128)S(1)} %get-tuple-element.122, bf16[8,16,3072]{2,1,0:T(8,128)(2,1)S(1)} %copy-done.1, f32[16,3072]{1,0:T(8,128)S(1)} %fusion.69), kind=kOutput, calls=%fused_computation.88 | convolution fusion | flops 102629376 | bytes 6488576 | tf_op jit(solution)/shard_map/tab,klta->kltb/dot_general | solution.py:81
  76.3 1.5 %collective-permute-start.2 = (f32[8,16,3,128]{3,1,0,2:T(8,128)S(1)}, f32[8,16,3,128]{3,1,0,2:T(8,128)S(1)}, u32[]{:S(2)}, u32[]{:S(2)}) collective-permute-start(f32[8,16,3,128]{3,1,0,2:T(8,128)S(1)} %slice.403), channel_id=1, source_target_pairs={{0,4},{4,8},{8,12},{12,16},{16,20},{20,24},{24,28},{28,0},{1,5},{5... | collective-permute-start | bytes 589832 | tf_op jit(solution)/shard_map/ppermute | solution.py:22
  77.8 0.1 slice.401
  78.0 0.0 copy-start.2
  78.0 6.7 %collective-permute-done.2 = f32[8,16,3,128]{3,1,0,2:T(8,128)S(1)} collective-permute-done((f32[8,16,3,128]{3,1,0,2:T(8,128)S(1)}, f32[8,16,3,128]{3,1,0,2:T(8,128)S(1)}, u32[]{:S(2)}, u32[]{:S(2)}) %collective-permute-start.2) | collective-permute-done | bytes 196640 | tf_op jit(solution)/shard_map/ppermute | solution.py:22
  84.7 1.1 %fusion.72 = (f32[8,16,3,128]{3,1,0,2:T(8,128)S(1)}, f32[8,16,24,128]{3,1,0,2:T(8,128)S(1)}) fusion(f32[8,16,24,128]{3,1,0,2:T(8,128)} %get-tuple-element.129, f32[8,16,24,128]{3,1,0,2:T(8,128)S(1)} %slice.401, f32[8,16,3,128]{3,1,0,2:T(8,128)S(1)} %collective-permute-done.2), kind=kLoop, calls=%fused_computation.97 | loop fusion | flops 49152 | bytes 983040 | tf_op jit(solution)/shard_map/slice | solution.py:91
  85.8 1.6 %collective-permute-start.3 = (f32[8,16,3,128]{3,1,0,2:T(8,128)S(1)}, f32[8,16,3,128]{3,1,0,2:T(8,128)S(1)}, u32[]{:S(2)}, u32[]{:S(2)}) collective-permute-start(f32[8,16,3,128]{3,1,0,2:T(8,128)S(1)} %get-tuple-element.110), channel_id=1, source_target_pairs={{0,28},{4,0},{8,4},{12,8},{16,12},{20,16},{24,20},{28,24},{1,29},{... | collective-permute-start | bytes 589832 | tf_op jit(solution)/shard_map/ppermute | solution.py:22
  87.4 1.5 %constant_dynamic-slice_fusion = f32[4,3072]{1,0:T(4,128)} fusion(f32[16,3072]{1,0:T(8,128)} %all-reduce.3.cloned.1.call-done, s32[]{:T(128)S(6)} %select_n.3), kind=kLoop, calls=%fused_computation.89 | loop fusion | bytes 98308 | tf_op jit(solution)/shard_map/dynamic_slice | solution.py:69
  88.9 2.6 %collective-permute-done.3 = f32[8,16,3,128]{3,1,0,2:T(8,128)S(1)} collective-permute-done((f32[8,16,3,128]{3,1,0,2:T(8,128)S(1)}, f32[8,16,3,128]{3,1,0,2:T(8,128)S(1)}, u32[]{:S(2)}, u32[]{:S(2)}) %collective-permute-start.3) | collective-permute-done | bytes 196640 | tf_op jit(solution)/shard_map/ppermute | solution.py:22
  91.6 0.0 copy-done.2
  91.6 2.1 %fusion = f32[8,16,3072]{2,1,0:T(8,128)} fusion(bf16[8,16,3072]{2,1,0:T(8,128)(2,1)S(1)} %copy-done.2, bf16[16,16]{1,0:T(8,128)(2,1)S(1)} %copy-done, f32[8,16,24,128]{3,1,0,2:T(8,128)S(1)} %fusion.67), kind=kOutput, calls=%fused_computation.1 | convolution fusion | flops 76283904 | bytes 3932672 | tf_op jit(solution)/shard_map/ml,kmh->klh/dot_general | solution.py:99
  (6 shorter events, 0.1 us)
Async XLA Ops:
  7.2 0.7 copy-start
  7.2 8.3 %copy-start.5 = (s32[24,7]{0,1:T(8,128)S(1)}, s32[24,7]{0,1:T(8,128)}, u32[]{:S(2)}) copy-start(s32[24,7]{0,1:T(8,128)} %param.29) | copy-start | bytes 2020
  7.2 60.4 %all-reduce.3.cloned.1.call-start = ((), (), s32[]{:S(2)}) async-start(), calls=%async_computation | async-start | bytes 393216 | tf_op jit(solution)/shard_map/psum | solution.py:68
  9.4 9.0 %collective-permute-start = (bf16[8,16,384]{2,1,0:T(8,128)(2,1)S(1)}, bf16[8,16,384]{2,1,0:T(8,128)(2,1)S(1)}, u32[]{:S(2)}, u32[]{:S(2)}) collective-permute-start(bf16[8,16,384]{2,1,0:T(8,128)(2,1)S(1)} %get-tuple-element.119), channel_id=1, source_target_pairs={{0,4},{4,8},{8,12},{12,16},{16,20},{20,24},{24,28},{28,0},{1,5},{5... | collective-permute-start | bytes 294920 | tf_op jit(solution)/shard_map/ppermute | solution.py:14
  12.4 6.7 %collective-permute-start.1 = (bf16[8,16,384]{2,1,0:T(8,128)(2,1)S(1)}, bf16[8,16,384]{2,1,0:T(8,128)(2,1)S(1)}, u32[]{:S(2)}, u32[]{:S(2)}) collective-permute-start(bf16[8,16,384]{2,1,0:T(8,128)(2,1)S(1)} %get-tuple-element.120), channel_id=1, source_target_pairs={{4,0},{8,4},{12,8},{16,12},{20,16},{24,20},{28,24},{0,28},{5,1},{9... | collective-permute-start | bytes 294920 | tf_op jit(solution)/shard_map/ppermute | solution.py:15
  32.0 2.3 %copy-start.1 = (bf16[8,16,3072]{2,1,0:T(8,128)(2,1)S(1)}, bf16[8,16,3072]{2,1,0:T(8,128)(2,1)}, u32[]{:S(2)}) copy-start(bf16[8,16,3072]{2,1,0:T(8,128)(2,1)} %param.26) | copy-start | bytes 2359300
  34.3 33.2 %copy-start.3 = (f32[16,3072]{1,0:T(8,128)S(1)}, f32[16,3072]{1,0:T(8,128)}, u32[]{:S(2)}) copy-start(f32[16,3072]{1,0:T(8,128)} %param.31) | copy-start | bytes 589828
  34.4 33.2 %copy-start.4 = (f32[16,3072]{1,0:T(8,128)S(1)}, f32[16,3072]{1,0:T(8,128)}, u32[]{:S(2)}) copy-start(f32[16,3072]{1,0:T(8,128)} %param.30) | copy-start | bytes 589828
  68.6 3.7 %slice-start = ((s8[5505024]{0:T(1024)(128)(4,1)}), s8[4194304]{0:T(1024)(128)(4,1)S(1)}, s32[]{:S(2)}) async-start(s8[5505024]{0:T(1024)(128)(4,1)} %bitcast.160), calls=%async_computation.1 | async-start | bytes 8388608
  70.3 2.0 %slice-start.1 = ((s8[5505024]{0:T(1024)(128)(4,1)}), s8[1310720]{0:T(1024)(128)(4,1)S(1)}, s32[]{:S(2)}) async-start(s8[5505024]{0:T(1024)(128)(4,1)} %bitcast.160), calls=%async_computation.2 | async-start | bytes 2621440
  76.3 8.4 %collective-permute-start.2 = (f32[8,16,3,128]{3,1,0,2:T(8,128)S(1)}, f32[8,16,3,128]{3,1,0,2:T(8,128)S(1)}, u32[]{:S(2)}, u32[]{:S(2)}) collective-permute-start(f32[8,16,3,128]{3,1,0,2:T(8,128)S(1)} %slice.403), channel_id=1, source_target_pairs={{0,4},{4,8},{8,12},{12,16},{16,20},{20,24},{24,28},{28,0},{1,5},{5... | collective-permute-start | bytes 589832 | tf_op jit(solution)/shard_map/ppermute | solution.py:22
  78.0 13.6 %copy-start.2 = (bf16[8,16,3072]{2,1,0:T(8,128)(2,1)S(1)}, bf16[8,16,3072]{2,1,0:T(8,128)(2,1)}, u32[]{:S(2)}) copy-start(bf16[8,16,3072]{2,1,0:T(8,128)(2,1)} %param.25) | copy-start | bytes 2359300
  85.8 5.7 %collective-permute-start.3 = (f32[8,16,3,128]{3,1,0,2:T(8,128)S(1)}, f32[8,16,3,128]{3,1,0,2:T(8,128)S(1)}, u32[]{:S(2)}, u32[]{:S(2)}) collective-permute-start(f32[8,16,3,128]{3,1,0,2:T(8,128)S(1)} %get-tuple-element.110), channel_id=1, source_target_pairs={{0,28},{4,0},{8,4},{12,8},{16,12},{20,16},{24,20},{28,24},{1,29},{... | collective-permute-start | bytes 589832 | tf_op jit(solution)/shard_map/ppermute | solution.py:22
Sparse Core Ops, SparseCore 0:
  35.4 32.1 all-reduce.2
where the time goes:
time: 101 us
  waiting for transfers between devices  45.3 us (45%)
  matrix products  24.1 us (24%)
  between operations  14.3 us (14%)
  starting transfers between devices  9.29 us (9%)
  local copies, waits for them, and re-layouts  4.6 us (5%)
  other arithmetic  3.06 us (3%)
    psum x1, waiting for transfers between devices, on_device(): summed_total = lax.psum(partial_sum, 'mem')  32.3 us
    dot_general x7, matrix products, apply_rows(): jnp.einsum('tab,kltb->klta', blocks[:, slot_index], source, preferred_ele...  13.1 us
    ppermute x2, waiting for transfers between devices, passed_along(): lax.ppermute(value, axis, [(i, (i + by) % length) for i in range(length)])  9.32 us
    dot_general x7, matrix products, on_device(): jnp.einsum('tab,klta->kltb', blocks[:, slot_index], weighted_tiles, prefe...  7.37 us
    ppermute x2, starting transfers between devices, passed_along(): lax.ppermute(value, axis, [(i, (i + by) % length) for i in range(length)])  3.13 us
    ppermute x1, starting transfers between devices, padded_2(): after = lax.ppermute(first, axis, down)  3.1 us
    ppermute x1, starting transfers between devices, padded_2(): before = lax.ppermute(last, axis, up)  3.02 us
    ppermute x1, waiting for transfers between devices, padded_2(): before = lax.ppermute(last, axis, up)  2.82 us
  transfers between devices with their start and end apart: 5, of which 5 were waited for; matrix products, arithmetic and copies ran while one was open for 2% of the time, Pallas kernels for 0%

commit v1 on v0

--- a/solution.py
+++ b/solution.py
@@ -65,7 +65,10 @@
     partial_sum = jnp.sum(ensemble.astype(jnp.float32) * localized, axis=0)
     row_count = level_count // lax.axis_size("mem")
     first_row = lax.axis_index("mem") * row_count
-    summed_total = lax.psum(partial_sum, "mem")
+    devices, summed_total = (lax.axis_size("mem"), partial_sum)
+    for hop in [1 << k for k in range(devices.bit_length() - 1)]:
+        pairs = [(i_2, i_2 ^ hop) for i_2 in range(devices)]
+        summed_total = summed_total + lax.ppermute(summed_total, "mem", pairs)
     increment = lax.dynamic_slice_in_dim(summed_total, first_row, row_count, 0)
     depart = (obs_precision * (summed_total - background)).astype(jnp.bfloat16)
     weighted = (ensemble.astype(jnp.float32) * depart.astype(jnp.float32)[None]).astype(

time: 101 us -> 57.3 us (0.57)
  waiting for transfers between devices: 45.3 us -> 22.3 us
  between operations: 14.3 us -> 0.9 us
  matrix products: 24.1 us -> 17.4 us
  other arithmetic: 3.06 us -> 2.05 us
    psum x1 -> x0, waiting for transfers between devices: 32.3 us -> none  [on_device(): summed_total = lax.psum(partial_sum, 'mem')]
    ppermute x0 -> x2, waiting for transfers between devices: none -> 6.88 us  [on_device(): summed_total = summed_total + lax.ppermute(summed_total, 'mem', pairs)]
    dot_general x7, matrix products: 7.37 us -> 3.73 us  [on_device(): jnp.einsum('tab,klta->kltb', blocks[:, slot_index], weighted_tiles, prefe...]
    dot_general x7, matrix products: 13.1 us -> 10 us  [apply_rows(): jnp.einsum('tab,kltb->klta', blocks[:, slot_index], source, preferred_ele...]
    ppermute x2, waiting for transfers between devices: 9.32 us -> 11.8 us  [passed_along(): lax.ppermute(value, axis, [(i, (i + by) % length) for i in range(length)])]
    ppermute x2, starting transfers between devices: 3.13 us -> 1.36 us  [passed_along(): lax.ppermute(value, axis, [(i, (i + by) % length) for i in range(length)])]
    ppermute x0 -> x2, starting transfers between devices: none -> 1.63 us  [on_device(): summed_total = summed_total + lax.ppermute(summed_total, 'mem', pairs)]
  transfers between devices with their start and end apart: 5 -> 6, of which waited for: 5 -> 6; matrix products, arithmetic and copies ran while one was open for 2% -> 3% of each run, Pallas kernels for 0% -> 0%
where the time goes in v1:
time: 57.3 us; the launch traced here: 57 us
  waiting for transfers between devices  22.3 us (39%)
  matrix products  17.4 us (30%)
  starting transfers between devices  9.1 us (16%)
  local copies, waits for them, and re-layouts  5.31 us (9%)
  other arithmetic  2.05 us (4%)
  between operations  0.9 us (2%)
    ppermute x2, waiting for transfers between devices, passed_along(): lax.ppermute(value, axis, [(i, (i + by) % length) for i in range(length)])  11.8 us
    dot_general x7, matrix products, apply_rows(): jnp.einsum('tab,kltb->klta', blocks[:, slot_index], source, preferred_ele...  10 us
    ppermute x2, waiting for transfers between devices, on_device(): summed_total = summed_total + lax.ppermute(summed_total, 'mem', pairs)  6.88 us
    dot_general x7, matrix products, on_device(): jnp.einsum('tab,klta->kltb', blocks[:, slot_index], weighted_tiles, prefe...  3.73 us
    ppermute x1, starting transfers between devices, padded_2(): after = lax.ppermute(first, axis, down)  3.1 us
    ppermute x1, starting transfers between devices, padded_2(): before = lax.ppermute(last, axis, up)  3.02 us
    ppermute x1, waiting for transfers between devices, padded_2(): before = lax.ppermute(last, axis, up)  2.82 us
    dot_general x1, matrix products, on_device(): jnp.einsum('ml,kmh->klh', vertical_loc.astype(jnp.float32), adjoint, prec...  2.15 us
  transfers between devices with their start and end apart: 6, of which 6 were waited for; matrix products, arithmetic and copies ran while one was open for 3% of the time, Pallas kernels for 0%

profile of v1, /device:TPU:0, one launch (start us, length us, event | category | flops | bytes accessed | tf_op | source)
XLA Modules:
  0.0 57.0 jit_solution(7576305399718632632)
XLA Ops:
  0.6 0.0 copy-start
  0.6 0.0 copy-start.5
  0.7 0.7 %copy-done = bf16[16,16]{1,0:T(8,128)(2,1)S(1)} copy-done((bf16[16,16]{1,0:T(8,128)(2,1)S(1)}, bf16[16,16]{1,0:T(8,128)(2,1)}, u32[]{:S(2)}) %copy-start) | copy-done | bytes 536
  1.3 1.5 %fusion.1 = bf16[8,16,3072]{2,1,0:T(8,128)(2,1)S(1)} fusion(bf16[8,16,3072]{2,1,0:T(8,128)(2,1)} %param.25, bf16[16,16]{1,0:T(8,128)(2,1)S(1)} %copy-done), kind=kOutput, calls=%fused_computation.3 | convolution fusion | flops 12976128 | bytes 1573376 | tf_op jit(solution)/shard_map/lm,kmh->klh/dot_general | solution.py:58
  2.8 3.0 %collective-permute-start = (bf16[8,16,384]{2,1,0:T(8,128)(2,1)S(1)}, bf16[8,16,384]{2,1,0:T(8,128)(2,1)S(1)}, u32[]{:S(2)}, u32[]{:S(2)}) collective-permute-start(bf16[8,16,384]{2,1,0:T(8,128)(2,1)S(1)} %get-tuple-element.121), channel_id=1, source_target_pairs={{0,4},{4,8},{8,12},{12,16},{16,20},{20,24},{24,28},{28,0},{1,5},{5... | collective-permute-start | bytes 294920 | tf_op jit(solution)/shard_map/ppermute | solution.py:14
  5.8 3.1 %collective-permute-start.1 = (bf16[8,16,384]{2,1,0:T(8,128)(2,1)S(1)}, bf16[8,16,384]{2,1,0:T(8,128)(2,1)S(1)}, u32[]{:S(2)}, u32[]{:S(2)}) collective-permute-start(bf16[8,16,384]{2,1,0:T(8,128)(2,1)S(1)} %get-tuple-element.122), channel_id=1, source_target_pairs={{4,0},{8,4},{12,8},{16,12},{20,16},{24,20},{28,24},{0,28},{5,1},{9... | collective-permute-start | bytes 294920 | tf_op jit(solution)/shard_map/ppermute | solution.py:15
  9.0 0.0 copy-done.5
  9.0 2.8 %collective-permute-done = bf16[8,16,384]{2,1,0:T(8,128)(2,1)S(1)} collective-permute-done((bf16[8,16,384]{2,1,0:T(8,128)(2,1)S(1)}, bf16[8,16,384]{2,1,0:T(8,128)(2,1)S(1)}, u32[]{:S(2)}, u32[]{:S(2)}) %collective-permute-start) | collective-permute-done | bytes 98336 | tf_op jit(solution)/shard_map/ppermute | solution.py:14
  11.8 0.8 %collective-permute-done.1 = bf16[8,16,384]{2,1,0:T(8,128)(2,1)S(1)} collective-permute-done((bf16[8,16,384]{2,1,0:T(8,128)(2,1)S(1)}, bf16[8,16,384]{2,1,0:T(8,128)(2,1)S(1)}, u32[]{:S(2)}, u32[]{:S(2)}) %collective-permute-start.1) | collective-permute-done | bytes 98336 | tf_op jit(solution)/shard_map/ppermute | solution.py:15
  12.6 0.1 pad_maximum_fusion
  12.6 0.6 %reshape.325 = bf16[8,16,30,128]{3,2,1,0:T(8,128)(2,1)S(1)} reshape(bf16[8,16,3840]{2,1,0:T(8,128)(2,1)S(1)} %pad_maximum_fusion) | data formatting | bytes 1966080 | tf_op jit(solution)/shard_map/reshape | solution.py:37
  13.2 0.0 slice-start
  13.3 1.4 %fusion.73 = (bf16[8,16,24,128]{3,2,1,0:T(8,128)(2,1)S(1)}, bf16[8,16,24,128]{3,2,1,0:T(8,128)(2,1)S(1)}, bf16[8,16,24,128]{3,2,1,0:T(8,128)(2,1)S(1)}, bf16[8,1...) fusion(bf16[8,16,30,128]{3,2,1,0:T(8,128)(2,1)S(1)} %reshape.325), kind=kLoop, calls=%fused_computation.98 | loop fusion | bytes 11010048 | tf_op jit(solution)/shard_map/slice | solution.py:45
  14.7 0.0 slice-start.1
  14.7 1.9 %fusion.22 = f32[24,8,16,128]{3,2,1,0:T(8,128)S(1)} fusion(bf16[8,16,24,128]{3,2,1,0:T(8,128)(2,1)S(1)} %get-tuple-element.115, bf16[24,7,128,128]{3,2,1,0:T(8,128)(2,1)} %param.28), kind=kOutput, calls=%fused_computation.35 | convolution fusion | flops 100663296 | bytes 3145728 | tf_op jit(solution)/shard_map/tab,kltb->klta/dot_general | solution.py:46
  16.7 1.8 %fusion.25 = f32[24,8,16,128]{3,2,1,0:T(8,128)S(1)} fusion(bf16[8,16,24,128]{3,2,1,0:T(8,128)(2,1)S(1)} %get-tuple-element.116, bf16[24,7,128,128]{3,2,1,0:T(8,128)(2,1)} %param.28), kind=kOutput, calls=%fused_computation.38 | convolution fusion | flops 100663296 | bytes 3145728 | tf_op jit(solution)/shard_map/tab,kltb->klta/dot_general | solution.py:46
  18.5 1.8 %fusion.28 = f32[24,8,16,128]{3,2,1,0:T(8,128)S(1)} fusion(bf16[8,16,24,128]{3,2,1,0:T(8,128)(2,1)S(1)} %get-tuple-element.117, bf16[24,7,128,128]{3,2,1,0:T(8,128)(2,1)} %param.28), kind=kOutput, calls=%fused_computation.41 | convolution fusion | flops 100663296 | bytes 3145728 | tf_op jit(solution)/shard_map/tab,kltb->klta/dot_general | solution.py:46
  20.3 1.8 %fusion.31 = f32[24,8,16,128]{3,2,1,0:T(8,128)S(1)} fusion(bf16[8,16,24,128]{3,2,1,0:T(8,128)(2,1)S(1)} %get-tuple-element.118, bf16[24,7,128,128]{3,2,1,0:T(8,128)(2,1)} %param.28), kind=kOutput, calls=%fused_computation.44 | convolution fusion | flops 100663296 | bytes 3145728 | tf_op jit(solution)/shard_map/tab,kltb->klta/dot_general | solution.py:46
  22.1 0.0 slice-done
  22.1 0.0 slice-done.1
  22.1 0.7 %fusion.34 = f32[24,8,16,128]{3,2,1,0:T(8,128)S(1)} fusion(bf16[8,16,24,128]{3,2,1,0:T(8,128)(2,1)S(1)} %get-tuple-element.119, bf16[24,7,128,128]{3,2,1,0:T(8,128)(2,1)S(1)} %bitcast.161), kind=kOutput, calls=%fused_computation.47 | convolution fusion | flops 100663296 | bytes 3145728 | tf_op jit(solution)/shard_map/tab,kltb->klta/dot_general | solution.py:46
  22.8 0.7 %fusion.37 = f32[24,8,16,128]{3,2,1,0:T(8,128)S(1)} fusion(bf16[8,16,24,128]{3,2,1,0:T(8,128)(2,1)S(1)} %get-tuple-element.120, bf16[24,7,128,128]{3,2,1,0:T(8,128)(2,1)S(1)} %bitcast.161), kind=kOutput, calls=%fused_computation.50 | convolution fusion | flops 100663296 | bytes 3145728 | tf_op jit(solution)/shard_map/tab,kltb->klta/dot_general | solution.py:46
  23.4 0.0 copy-start.1
  23.4 1.4 %add_bitcast_fusion = f32[24,8,2,8,128]{4,3,2,1,0:T(8,128)S(1)} fusion(f32[24,8,16,128]{3,2,1,0:T(8,128)S(1)} %fusion.22, f32[24,8,16,128]{3,2,1,0:T(8,128)S(1)} %fusion.25, f32[24,8,16,128]{3,2,1,0:T(8,128)S(1)} %fusion.28, f32[24,8,16,128]{3,2,1,0:T(8,128)S(1)} %fusion.31, f32[24,8,16,128]{3,2,1,0:T(8,128)S(1)} %fusion.34, ...), kind=kOutput, calls=%fused_computation.21 | convolution fusion | flops 105775104 | bytes 12586496 | tf_op jit(solution)/shard_map/tab,kltb->klta/dot_general | solution.py:46
  24.8 0.0 copy-done.1
  24.8 0.0 copy-start.3
  24.8 0.0 copy-start.4
  24.8 0.2 fusion.2
  25.0 0.1 collective-permute-start.2
  25.1 1.4 %collective-permute-done.2 = f32[16,3072]{1,0:T(8,128)S(1)} collective-permute-done((f32[16,3072]{1,0:T(8,128)S(1)}, f32[16,3072]{1,0:T(8,128)S(1)}, u32[]{:S(2)}, u32[]{:S(2)}) %collective-permute-start.2) | collective-permute-done | bytes 196640 | tf_op jit(solution)/shard_map/ppermute | solution.py:71
  26.6 1.6 %collective-permute-start.3 = (f32[16,3072]{1,0:T(8,128)S(1)}, f32[16,3072]{1,0:T(8,128)S(1)}, u32[]{:S(2)}, u32[]{:S(2)}) collective-permute-start(f32[16,3072]{1,0:T(8,128)S(1)} %add.105), channel_id=1, source_target_pairs={{0,2},{1,3},{2,0},{3,1},{4,6},{5,7},{6,4},{7,5},{8,10},{9,11},{10,... | collective-permute-start | bytes 589832 | tf_op jit(solution)/shard_map/ppermute | solution.py:71
  28.1 5.5 %collective-permute-done.3 = f32[16,3072]{1,0:T(8,128)S(1)} collective-permute-done((f32[16,3072]{1,0:T(8,128)S(1)}, f32[16,3072]{1,0:T(8,128)S(1)}, u32[]{:S(2)}, u32[]{:S(2)}) %collective-permute-start.3) | collective-permute-done | bytes 196640 | tf_op jit(solution)/shard_map/ppermute | solution.py:71
  33.6 0.0 copy-done.3
  33.6 0.0 copy-done.4
  33.6 0.7 %fusion.69 = (f32[16,3072]{1,0:T(8,128)S(1)}, f32[16,3072]{1,0:T(8,128)}) fusion(f32[16,3072]{1,0:T(8,128)S(1)} %copy-done.3, f32[16,3072]{1,0:T(8,128)S(1)} %copy-done.4, f32[16,3072]{1,0:T(8,128)S(1)} %add.105, f32[16,3072]{1,0:T(8,128)S(1)} %collective-permute-done.3), kind=kLoop, calls=%fused_computation.85 | loop fusion | flops 245760 | bytes 1179648 | tf_op jit(solution)/shard_map/convert_element_type | solution.py:74
  34.3 0.4 multiply_bitcast_fusion
  34.7 0.2 scatter-add.30
  34.9 0.5 fusion.10
  35.5 0.5 fusion.9
  36.0 0.6 fusion.8
  36.6 0.6 fusion.7
  37.1 0.5 fusion.6
  37.7 0.6 %constant_dynamic-update-slice_fusion = (f32[8,16,30,128]{3,1,0,2:T(8,128)S(1)}, f32[8,16,24,128]{3,1,0,2:T(8,128)S(1)}) fusion(f32[8,16,30,128]{3,1,0,2:T(8,128)S(1)} %fusion.6, bf16[24,7,128,128]{3,2,1,0:T(8,128)(2,1)S(1)} %bitcast.161, f32[24]{0:T(128)S(1)} %get-tuple-element.124, bf16[8,16,3072]{2,1,0:T(8,128)(2,1)S(1)} %copy-done.1, ...), kind=kOutput, calls=%fused_computation.88 | convolution fusion | flops 102629376 | bytes 6488576 | tf_op jit(solution)/shard_map/tab,klta->kltb/dot_general | solution.py:84
  38.3 0.7 %slice.403 = f32[8,16,3,128]{3,1,0,2:T(8,128)} slice(f32[8,16,30,128]{3,1,0,2:T(8,128)S(1)} %get-tuple-element.130), slice={[0:8], [0:16], [27:30], [0:128]} | slice | bytes 393216 | tf_op jit(solution)/shard_map/slice | solution.py:95
  39.0 0.3 collective-permute-start.4
  39.3 0.1 slice.401
  39.5 0.0 copy-start.2
  39.5 8.6 %collective-permute-done.4 = f32[8,16,3,128]{3,1,0,2:T(8,128)} collective-permute-done((f32[8,16,3,128]{3,1,0,2:T(8,128)}, f32[8,16,3,128]{3,1,0,2:T(8,128)}, u32[]{:S(2)}, u32[]{:S(2)}) %collective-permute-start.4) | collective-permute-done | bytes 196640 | tf_op jit(solution)/shard_map/ppermute | solution.py:22
  48.1 1.0 %fusion.72 = (f32[8,16,3,128]{3,1,0,2:T(8,128)S(1)}, f32[8,16,24,128]{3,1,0,2:T(8,128)S(1)}) fusion(f32[8,16,24,128]{3,1,0,2:T(8,128)S(1)} %get-tuple-element.131, f32[8,16,24,128]{3,1,0,2:T(8,128)S(1)} %slice.401, f32[8,16,3,128]{3,1,0,2:T(8,128)} %collective-permute-done.4), kind=kLoop, calls=%fused_computation.97 | loop fusion | flops 49152 | bytes 983040 | tf_op jit(solution)/shard_map/slice | solution.py:94
  49.1 1.0 %collective-permute-start.5 = (f32[8,16,3,128]{3,1,0,2:T(8,128)S(1)}, f32[8,16,3,128]{3,1,0,2:T(8,128)S(1)}, u32[]{:S(2)}, u32[]{:S(2)}) collective-permute-start(f32[8,16,3,128]{3,1,0,2:T(8,128)S(1)} %get-tuple-element.112), channel_id=1, source_target_pairs={{0,28},{4,0},{8,4},{12,8},{16,12},{20,16},{24,20},{28,24},{1,29},{... | collective-permute-start | bytes 589832 | tf_op jit(solution)/shard_map/ppermute | solution.py:22
  50.1 1.5 %constant_dynamic-slice_fusion = f32[4,3072]{1,0:T(4,128)} fusion(f32[16,3072]{1,0:T(8,128)} %get-tuple-element.111, s32[]{:T(128)S(6)} %select_n.3), kind=kLoop, calls=%fused_computation.89 | loop fusion | bytes 98308 | tf_op jit(solution)/shard_map/dynamic_slice | solution.py:72
  51.6 3.2 %collective-permute-done.5 = f32[8,16,3,128]{3,1,0,2:T(8,128)S(1)} collective-permute-done((f32[8,16,3,128]{3,1,0,2:T(8,128)S(1)}, f32[8,16,3,128]{3,1,0,2:T(8,128)S(1)}, u32[]{:S(2)}, u32[]{:S(2)}) %collective-permute-start.5) | collective-permute-done | bytes 196640 | tf_op jit(solution)/shard_map/ppermute | solution.py:22
  54.8 0.0 copy-done.2
  54.9 2.1 %fusion = f32[8,16,3072]{2,1,0:T(8,128)} fusion(bf16[8,16,3072]{2,1,0:T(8,128)(2,1)S(1)} %copy-done.2, bf16[16,16]{1,0:T(8,128)(2,1)S(1)} %copy-done, f32[8,16,24,128]{3,1,0,2:T(8,128)S(1)} %fusion.67), kind=kOutput, calls=%fused_computation.1 | convolution fusion | flops 76283904 | bytes 3932672 | tf_op jit(solution)/shard_map/ml,kmh->klh/dot_general | solution.py:102
  (6 shorter events, 0.1 us)
Async XLA Ops:
  0.6 0.7 %copy-start = (bf16[16,16]{1,0:T(8,128)(2,1)S(1)}, bf16[16,16]{1,0:T(8,128)(2,1)}, u32[]{:S(2)}) copy-start(bf16[16,16]{1,0:T(8,128)(2,1)} %param.27) | copy-start | bytes 1540
  0.6 8.3 %copy-start.5 = (s32[24,7]{0,1:T(8,128)S(1)}, s32[24,7]{0,1:T(8,128)}, u32[]{:S(2)}) copy-start(s32[24,7]{0,1:T(8,128)} %param.29) | copy-start | bytes 2020
  2.8 9.0 %collective-permute-start = (bf16[8,16,384]{2,1,0:T(8,128)(2,1)S(1)}, bf16[8,16,384]{2,1,0:T(8,128)(2,1)S(1)}, u32[]{:S(2)}, u32[]{:S(2)}) collective-permute-start(bf16[8,16,384]{2,1,0:T(8,128)(2,1)S(1)} %get-tuple-element.121), channel_id=1, source_target_pairs={{0,4},{4,8},{8,12},{12,16},{16,20},{20,24},{24,28},{28,0},{1,5},{5... | collective-permute-start | bytes 294920 | tf_op jit(solution)/shard_map/ppermute | solution.py:14
  5.8 6.7 %collective-permute-start.1 = (bf16[8,16,384]{2,1,0:T(8,128)(2,1)S(1)}, bf16[8,16,384]{2,1,0:T(8,128)(2,1)S(1)}, u32[]{:S(2)}, u32[]{:S(2)}) collective-permute-start(bf16[8,16,384]{2,1,0:T(8,128)(2,1)S(1)} %get-tuple-element.122), channel_id=1, source_target_pairs={{4,0},{8,4},{12,8},{16,12},{20,16},{24,20},{28,24},{0,28},{5,1},{9... | collective-permute-start | bytes 294920 | tf_op jit(solution)/shard_map/ppermute | solution.py:15
  13.2 8.8 %slice-start = ((s8[5505024]{0:T(1024)(128)(4,1)}), s8[1310720]{0:T(1024)(128)(4,1)S(1)}, s32[]{:S(2)}) async-start(s8[5505024]{0:T(1024)(128)(4,1)} %bitcast.160), calls=%async_computation | async-start | bytes 2621440
  14.7 7.4 %slice-start.1 = ((s8[5505024]{0:T(1024)(128)(4,1)}), s8[4194304]{0:T(1024)(128)(4,1)S(1)}, s32[]{:S(2)}) async-start(s8[5505024]{0:T(1024)(128)(4,1)} %bitcast.160), calls=%async_computation.1 | async-start | bytes 8388608
  23.4 1.4 %copy-start.1 = (bf16[8,16,3072]{2,1,0:T(8,128)(2,1)S(1)}, bf16[8,16,3072]{2,1,0:T(8,128)(2,1)}, u32[]{:S(2)}) copy-start(bf16[8,16,3072]{2,1,0:T(8,128)(2,1)} %param.26) | copy-start | bytes 2359300
  24.8 8.8 %copy-start.3 = (f32[16,3072]{1,0:T(8,128)S(1)}, f32[16,3072]{1,0:T(8,128)}, u32[]{:S(2)}) copy-start(f32[16,3072]{1,0:T(8,128)} %param.31) | copy-start | bytes 589828
  24.8 8.8 %copy-start.4 = (f32[16,3072]{1,0:T(8,128)S(1)}, f32[16,3072]{1,0:T(8,128)}, u32[]{:S(2)}) copy-start(f32[16,3072]{1,0:T(8,128)} %param.30) | copy-start | bytes 589828
  25.0 1.5 %collective-permute-start.2 = (f32[16,3072]{1,0:T(8,128)S(1)}, f32[16,3072]{1,0:T(8,128)S(1)}, u32[]{:S(2)}, u32[]{:S(2)}) collective-permute-start(f32[16,3072]{1,0:T(8,128)S(1)} %fusion.2), channel_id=1, source_target_pairs={{0,1},{1,0},{2,3},{3,2},{4,5},{5,4},{6,7},{7,6},{8,9},{9,8},{10,11... | collective-permute-start | bytes 589832 | tf_op jit(solution)/shard_map/ppermute | solution.py:71
  26.6 7.0 %collective-permute-start.3 = (f32[16,3072]{1,0:T(8,128)S(1)}, f32[16,3072]{1,0:T(8,128)S(1)}, u32[]{:S(2)}, u32[]{:S(2)}) collective-permute-start(f32[16,3072]{1,0:T(8,128)S(1)} %add.105), channel_id=1, source_target_pairs={{0,2},{1,3},{2,0},{3,1},{4,6},{5,7},{6,4},{7,5},{8,10},{9,11},{10,... | collective-permute-start | bytes 589832 | tf_op jit(solution)/shard_map/ppermute | solution.py:71
  39.0 9.1 %collective-permute-start.4 = (f32[8,16,3,128]{3,1,0,2:T(8,128)}, f32[8,16,3,128]{3,1,0,2:T(8,128)}, u32[]{:S(2)}, u32[]{:S(2)}) collective-permute-start(f32[8,16,3,128]{3,1,0,2:T(8,128)} %slice.403), channel_id=1, source_target_pairs={{0,4},{4,8},{8,12},{12,16},{16,20},{20,24},{24,28},{28,0},{1,5},{5... | collective-permute-start | bytes 589832 | tf_op jit(solution)/shard_map/ppermute | solution.py:22
  39.5 15.4 %copy-start.2 = (bf16[8,16,3072]{2,1,0:T(8,128)(2,1)S(1)}, bf16[8,16,3072]{2,1,0:T(8,128)(2,1)}, u32[]{:S(2)}) copy-start(bf16[8,16,3072]{2,1,0:T(8,128)(2,1)} %param.25) | copy-start | bytes 2359300
  49.1 5.7 %collective-permute-start.5 = (f32[8,16,3,128]{3,1,0,2:T(8,128)S(1)}, f32[8,16,3,128]{3,1,0,2:T(8,128)S(1)}, u32[]{:S(2)}, u32[]{:S(2)}) collective-permute-start(f32[8,16,3,128]{3,1,0,2:T(8,128)S(1)} %get-tuple-element.112), channel_id=1, source_target_pairs={{0,28},{4,0},{8,4},{12,8},{16,12},{20,16},{24,20},{28,24},{1,29},{... | collective-permute-start | bytes 589832 | tf_op jit(solution)/shard_map/ppermute | solution.py:22
